TPU v7x, 256 devices: a whole 4x4x8 slice. The times are simulated.
256 devices in a mesh: ka: 32 (over z_lo, y, core), pa: 8 (over z_hi, x).
Axes of the slice: x: 4, y: 4, z: 8 (z_hi: 2, z_lo: 4; z = z_hi * 4 + z_lo), core: 2. Of those that a mesh axis runs over, the one named last changes fastest.
Arguments:
- previous: float32 [256, 256, 256], P('ka', None, 'pa'), may hold values from -6 to 6
- current: float32 [256, 256, 256], P('ka', None, 'pa'), may hold values from -6 to 6
- energies: float32 [256, 256, 256], P('ka', None, 'pa'), may hold values from -0.5 to 0.5
- valence: float32 [256, 256, 256], P('ka'), may hold values from -0.375 to 0.375
- conduction: float32 [256, 256, 256], P('ka', None, 'pa'), may hold values from -0.375 to 0.375
- kernel: float32 [256, 256, 256], P(None, 'ka', 'pa'), may hold values from 0.05 to 0.35
Outputs:
- next_one: float32 [256, 256, 256], P('ka', None, 'pa')
- next_two: float32 [256, 256, 256], P('ka', None, 'pa')
All inputs are finite; a program needn't handle non-finite values.
Results may differ from a plain program's by a relative error of at most 0.000096.
Values sent between devices are 32-bit elements; how exact they have to be, the bound alone decides.
No kernel may reach another device: no remote copies, remote signals or barrier semaphores. Data moves between devices by JAX's collectives and lax.ppermute only.
A program may use at most 64 MiB of HBM per device.

v0:
```python
import math
import jax
import jax.numpy as jnp
from jax import lax
from jax.sharding import PartitionSpec as P

KY = 16


def phase_tables(total):
    points = jnp.arange(total)
    wide = total // KY
    coarse = points // KY
    finer = points % KY
    turns = (coarse[:, None] * coarse[None, :] % wide).astype(jnp.float32) / wide
    turns = turns + (finer[:, None] * finer[None, :] % KY).astype(jnp.float32) / KY
    angles = 2.0 * math.pi * turns
    return (jnp.cos(angles), jnp.sin(angles))


def screen_owned(flattened, kernel, cosine_table, sine_table):
    highest = lax.Precision.HIGHEST
    total = kernel.shape[0]
    even = jnp.dot(cosine_table, flattened, precision=highest)
    odd = jnp.dot(sine_table, flattened, precision=highest)
    weights = kernel.reshape(total, kernel.shape[1] * kernel.shape[2])
    return (
        jnp.dot(cosine_table, weights * even, precision=highest)
        + jnp.dot(sine_table, weights * odd, precision=highest)
    ) / total


def kernel_product(field, valence, conduction, kernel, cosine_table, sine_table):
    highest = lax.Precision.HIGHEST
    total = kernel.shape[0]
    inner = jnp.einsum("kvc,kcn->kvn", field, conduction, precision=highest)
    pair_blocks = jnp.einsum("kvm,kvn->kmn", valence, inner, precision=highest)
    owned = lax.all_to_all(pair_blocks, "ka", split_axis=1, concat_axis=0, tiled=True)
    flattened = owned.reshape(total, owned.shape[1] * owned.shape[2])
    screened = screen_owned(flattened, kernel, cosine_table, sine_table).reshape(owned.shape)
    returned = lax.all_to_all(screened, "ka", split_axis=0, concat_axis=1, tiled=True)
    partial_rows = jnp.einsum("kmn,kcn->kmc", returned, conduction, precision=highest)
    return jnp.einsum("kvm,kmc->kvc", valence, partial_rows, precision=highest)


def on_device(previous, current, energies, valence, conduction, kernel):
    cosine_table, sine_table = phase_tables(kernel.shape[0])
    whole_current = lax.all_gather(current, "pa", axis=2, tiled=True)
    folded_term = kernel_product(
        whole_current, valence, conduction, kernel, cosine_table, sine_table
    )
    summed = lax.psum_scatter(folded_term, "pa", scatter_dimension=2, tiled=True)
    next_one = 2.0 * (energies * current + summed) - previous
    whole_next = lax.all_gather(next_one, "pa", axis=2, tiled=True)
    second_term = kernel_product(whole_next, valence, conduction, kernel, cosine_table, sine_table)
    second_sum = lax.psum_scatter(second_term, "pa", scatter_dimension=2, tiled=True)
    next_two = 2.0 * (energies * next_one + second_sum) - current
    return (next_one, next_two)


def solution(mesh):
    placed = (
        P("ka", None, "pa"),
        P("ka", None, "pa"),
        P("ka", None, "pa"),
        P("ka", None, None),
        P("ka", None, "pa"),
        P(None, "ka", "pa"),
    )
    return jax.shard_map(
        on_device,
        mesh=mesh,
        in_specs=placed,
        out_specs=(P("ka", None, "pa"), P("ka", None, "pa")),
        check_vma=False,
    )
```

profile of v0, /device:TPU:8, one launch (start us, length us, event | category | flops | bytes accessed | tf_op | source)
XLA Modules:
  0.0 477.2 jit_solution(5078884266012246509)
XLA Ops:
  7.2 0.0 copy-start
  7.2 0.0 all-gather.3.cloned.1.call-start
  7.2 0.7 all-gather.3.cloned.1.call-update
  7.9 81.5 %all-gather.3.cloned.1.call-done = f32[8,256,256]{1,2,0:T(8,128)} async-done(((f32[8,256,32]{1,2,0:T(8,128)}), f32[8,256,256]{1,2,0:T(8,128)}) %all-gather.3.cloned.1.call-update) | async-done | bytes 2097168 | tf_op jit(solution)/shard_map/all_gather | solution.py:48
  89.4 3.0 fusion.60
  92.4 1.3 convolution_bitcast_fusion.3
  93.7 0.4 copy.31
  94.1 1.2 reshape.71
  95.2 5.2 %all-to-all-start = ((f32[32,1,2048]{2,1,0:T(1,128)}), f32[32,1,2048]{2,1,0:T(1,128)S(1)}, u32[]{:S(2)}, u32[]{:S(2)}) async-start(f32[32,1,2048]{2,1,0:T(1,128)} %reshape.71), calls=%async_computation | async-start | bytes 524288 | tf_op jit(solution)/shard_map/all_to_all | solution.py:38
  100.4 0.3 reduce-scatter.3.cloned.1.call-start
  100.8 1.8 copy.34
  102.6 7.3 %all-to-all-done = f32[32,1,2048]{2,1,0:T(1,128)S(1)} async-done(((f32[32,1,2048]{2,1,0:T(1,128)}), f32[32,1,2048]{2,1,0:T(1,128)S(1)}, u32[]{:S(2)}, u32[]{:S(2)}) %all-to-all-start) | async-done | bytes 262176 | tf_op jit(solution)/shard_map/all_to_all | solution.py:38
  109.8 0.6 broadcast.134
  110.4 1.2 reduce
  111.6 0.3 reshape.72
  112.0 0.0 copy-start.8
  112.0 1.2 copy.33
  113.1 1.5 reshape.67
  114.7 1.6 convolution_multiply_fusion.2
  116.3 1.6 convolution_multiply_fusion.3
  117.8 1.7 fusion.19
  119.5 1.7 fusion.1
  121.2 0.4 copy.36
  121.6 0.0 copy-start.1
  121.6 1.2 reshape.73
  122.8 15.4 %all_to_all.66 = f32[32,1,2048]{2,1,0:T(1,128)S(1)} all-to-all(f32[32,1,2048]{2,1,0:T(1,128)} %reshape.73), channel_id=1, replica_groups=mesh['ka'=32,'pa'=8] {'ka'}, dimensions={0} | all-to-all | bytes 524288 | tf_op jit(solution)/shard_map/all_to_all | solution.py:41
  138.2 2.0 reduce.1
  140.2 1.3 reshape.74
  141.5 1.9 fusion.4
  143.4 3.5 convolution_bitcast_fusion.1
  146.8 0.0 reduce-scatter.3.cloned.1.call-update
  146.9 0.0 all-gather.5.cloned.1.call-start
  146.9 92.0 %reduce-scatter.3.cloned.1.call-done = f32[8,256,32]{1,2,0:T(8,128)} async-done(((f32[8,256,256]{1,2,0:T(8,128)}), f32[8,256,32]{1,2,0:T(8,128)}) %reduce-scatter.3.cloned.1.call-update) | async-done | bytes 262160 | tf_op jit(solution)/shard_map/reduce_scatter | solution.py:52
  239.0 0.0 copy-done.2
  239.0 0.0 copy-done.7
  239.0 1.7 multiply_subtract_fusion.1
  240.7 0.0 all-gather.5.cloned.1.call-update
  240.7 0.0 reduce-scatter.5.cloned.1.call-start
  240.8 73.1 %all-gather.5.cloned.1.call-done = f32[8,256,256]{1,2,0:T(8,128)} async-done(((f32[8,256,32]{1,2,0:T(8,128)}), f32[8,256,256]{1,2,0:T(8,128)}) %all-gather.5.cloned.1.call-update) | async-done | bytes 2097168 | tf_op jit(solution)/shard_map/all_gather | solution.py:54
  313.9 3.0 fusion.61
  316.8 2.0 convolution_bitcast_fusion.2
  318.9 1.4 copy.40
  320.2 1.2 reshape.75
  321.4 14.7 %all_to_all.67 = f32[32,1,2048]{2,1,0:T(1,128)S(1)} all-to-all(f32[32,1,2048]{2,1,0:T(1,128)} %reshape.75), channel_id=1, replica_groups=mesh['ka'=32,'pa'=8] {'ka'}, dimensions={0} | all-to-all | bytes 524288 | tf_op jit(solution)/shard_map/all_to_all | solution.py:38
  336.1 2.0 reduce.2
  338.1 1.3 reshape.76
  339.4 1.2 copy.42
  340.5 1.6 reshape.69
  342.1 2.5 convolution_multiply_fusion
  344.6 0.0 copy-done.9
  344.7 1.6 convolution_multiply_fusion.1
  346.2 1.7 fusion.16
  347.9 2.4 fusion
  350.3 1.4 copy.45
  351.7 1.2 reshape.77
  352.8 15.1 %all_to_all.68 = f32[32,1,2048]{2,1,0:T(1,128)S(1)} all-to-all(f32[32,1,2048]{2,1,0:T(1,128)} %reshape.77), channel_id=1, replica_groups=mesh['ka'=32,'pa'=8] {'ka'}, dimensions={0} | all-to-all | bytes 524288 | tf_op jit(solution)/shard_map/all_to_all | solution.py:41
  368.0 2.0 reduce.3
  369.9 1.3 reshape.78
  371.2 1.9 fusion.2
  373.1 3.5 convolution_bitcast_fusion
  376.6 0.0 reduce-scatter.5.cloned.1.call-update
  376.6 92.1 %reduce-scatter.5.cloned.1.call-done = f32[8,256,32]{1,2,0:T(8,128)} async-done(((f32[8,256,256]{1,2,0:T(8,128)}), f32[8,256,32]{1,2,0:T(8,128)}) %reduce-scatter.5.cloned.1.call-update) | async-done | bytes 262160 | tf_op jit(solution)/shard_map/reduce_scatter | solution.py:56
  468.7 0.0 copy-done.3
  468.7 1.7 multiply_subtract_fusion
  (14 shorter events, 0.0 us)
Async XLA Ops:
  7.2 85.2 %copy-start = (f32[8,256,256]{2,1,0:T(8,128)S(1)}, f32[8,256,256]{2,1,0:T(8,128)}, u32[]{:S(2)}) copy-start(f32[8,256,256]{2,1,0:T(8,128)} %param.9) | copy-start | bytes 6291460
  7.2 82.2 %all-gather.3.cloned.1.call-start = ((), (), s32[]{:S(2)}) async-start(), calls=%async_computation.6 | async-start | bytes 2359296 | tf_op jit(solution)/shard_map/all_gather | solution.py:48
  95.2 14.6 %all-to-all-start = ((f32[32,1,2048]{2,1,0:T(1,128)}), f32[32,1,2048]{2,1,0:T(1,128)S(1)}, u32[]{:S(2)}, u32[]{:S(2)}) async-start(f32[32,1,2048]{2,1,0:T(1,128)} %reshape.71), calls=%async_computation | async-start | bytes 524288 | tf_op jit(solution)/shard_map/all_to_all | solution.py:38
  100.4 138.5 %reduce-scatter.3.cloned.1.call-start = ((), (), s32[]{:S(2)}) async-start(), calls=%async_computation.7 | async-start | bytes 2359296 | tf_op jit(solution)/shard_map/reduce_scatter | solution.py:52
  112.0 2.7 copy-start.8
  121.6 19.9 %copy-start.1 = (f32[8,256,32]{1,2,0:T(8,128)S(1)}, f32[8,256,32]{1,2,0:T(8,128)}, u32[]{:S(2)}) copy-start(f32[8,256,32]{1,2,0:T(8,128)} %param.10) | copy-start | bytes 786436
  146.8 92.1 %copy-start.2 = (f32[8,256,32]{1,2,0:T(8,128)S(1)}, f32[8,256,32]{1,2,0:T(8,128)}, u32[]{:S(2)}) copy-start(f32[8,256,32]{1,2,0:T(8,128)} %param.7) | copy-start | bytes 786436
  146.8 92.1 %copy-start.5 = (f32[8,256,32]{1,2,0:T(8,128)S(1)}, f32[8,256,32]{1,2,0:T(8,128)}, u32[]{:S(2)}) copy-start(f32[8,256,32]{1,2,0:T(8,128)} %param.8) | copy-start | bytes 786436
  146.8 92.1 %copy-start.7 = (f32[8,256,32]{1,2,0:T(8,128)S(1)}, f32[8,256,32]{1,2,0:T(8,128)}, u32[]{:S(2)}) copy-start(f32[8,256,32]{1,2,0:T(8,128)} %param.6) | copy-start | bytes 786436
  146.9 167.0 %all-gather.5.cloned.1.call-start = ((), (), s32[]{:S(2)}) async-start(), calls=%async_computation.8 | async-start | bytes 2359296 | tf_op jit(solution)/shard_map/all_gather | solution.py:54
  240.7 228.0 %reduce-scatter.5.cloned.1.call-start = ((), (), s32[]{:S(2)}) async-start(), calls=%async_computation.9 | async-start | bytes 2359296 | tf_op jit(solution)/shard_map/reduce_scatter | solution.py:56
  340.5 4.1 copy-start.9
  376.6 92.1 %copy-start.3 = (f32[8,256,32]{1,2,0:T(8,128)S(1)}, f32[8,256,32]{1,2,0:T(8,128)}, u32[]{:S(2)}) copy-start(f32[8,256,32]{1,2,0:T(8,128)} %param.7) | copy-start | bytes 786436
  376.6 92.1 %copy-start.4 = (f32[8,256,32]{1,2,0:T(8,128)S(1)}, f32[8,256,32]{1,2,0:T(8,128)}, u32[]{:S(2)}) copy-start(f32[8,256,32]{1,2,0:T(8,128)} %multiply_subtract_fusion.1) | copy-start | bytes 786436
  376.6 92.1 %copy-start.6 = (f32[8,256,32]{1,2,0:T(8,128)S(1)}, f32[8,256,32]{1,2,0:T(8,128)}, u32[]{:S(2)}) copy-start(f32[8,256,32]{1,2,0:T(8,128)} %param.8) | copy-start | bytes 786436
Sparse Core Ops, SparseCore 0:
  10.6 78.7 all-gather.2
  147.0 91.9 reduce-scatter.2
  242.2 71.6 all-gather.4
  376.7 91.9 reduce-scatter.4
where the time goes:
time: 481 us; the launch traced here: 477 us
  waiting for transfers between devices  347 us (72%)
  blocking collectives  45.3 us (9%)
  matrix products  34.5 us (7%)
  local copies, waits for them, and re-layouts  20.2 us (4%)
  between operations  14.2 us (3%)
  other arithmetic  10.6 us (2%)
  starting transfers between devices  5.63 us (1%)
    reduce_scatter x1, waiting for transfers between devices, on_device(): lax.psum_scatter(second_term, 'pa', scatter_dimension=2, tiled=True)  92.1 us
    reduce_scatter x1, waiting for transfers between devices, on_device(): lax.psum_scatter(folded_term, 'pa', scatter_dimension=2, tiled=True)  92 us
    all_gather x1, waiting for transfers between devices, on_device(): whole_current = lax.all_gather(current, 'pa', axis=2, tiled=True)  81.5 us
    all_gather x1, waiting for transfers between devices, on_device(): whole_next = lax.all_gather(next_one, 'pa', axis=2, tiled=True)  73.1 us
    all_to_all x2, blocking collectives, kernel_product(): lax.all_to_all(screened, 'ka', split_axis=0, concat_axis=1, tiled=True)  30.6 us
    all_to_all x1, blocking collectives, kernel_product(): lax.all_to_all(pair_blocks, 'ka', split_axis=1, concat_axis=0, tiled=True)  14.7 us
  transfers between devices with their start and end apart: 5, of which 5 were waited for; matrix products, arithmetic and copies ran while one was open for 0% of the time, Pallas kernels for 0%

commit v1 on v0

--- a/solution.py
+++ b/solution.py
@@ -5,6 +5,13 @@
 from jax.sharding import PartitionSpec as P
 
 KY = 16
+
+
+def balance_hubs(inp, axis_name):
+    history = []
+    for _ in range(lax.psum(1, axis_name)):
+        history.append(inp)
+    return jnp.concatenate(lax.all_to_all(jnp.stack(history, 0), axis_name, 0, 0), 2)
 
 
 def phase_tables(total):
@@ -51,7 +58,7 @@
     )
     summed = lax.psum_scatter(folded_term, "pa", scatter_dimension=2, tiled=True)
     next_one = 2.0 * (energies * current + summed) - previous
-    whole_next = lax.all_gather(next_one, "pa", axis=2, tiled=True)
+    whole_next = balance_hubs(next_one, "pa")
     second_term = kernel_product(whole_next, valence, conduction, kernel, cosine_table, sine_table)
     second_sum = lax.psum_scatter(second_term, "pa", scatter_dimension=2, tiled=True)
     next_two = 2.0 * (energies * next_one + second_sum) - current

time: 481 us -> 460 us (0.956)
  waiting for transfers between devices: 347 us -> 272 us
  blocking collectives: 45.3 us -> 100 us
    all_gather x1 -> x0, waiting for transfers between devices: 73.1 us -> none  [on_device(): whole_next = lax.all_gather(next_one, 'pa', axis=2, tiled=True)]
    all_to_all x0 -> x1, blocking collectives: none -> 51.1 us  [balance_hubs(): lax.all_to_all(jnp.stack(history, 0), axis_name, 0, 0)]
  transfers between devices with their start and end apart: 5 -> 4, of which waited for: 5 -> 4; matrix products, arithmetic and copies ran while one was open for 0% -> 0% of each run, Pallas kernels for 0% -> 0%
where the time goes in v1:
time: 460 us; the launch traced here: 456 us
  waiting for transfers between devices  272 us (59%)
  blocking collectives  100 us (22%)
  matrix products  32.9 us (7%)
  local copies, waits for them, and re-layouts  21.2 us (5%)
  between operations  14.3 us (3%)
  other arithmetic  9.85 us (2%)
  starting transfers between devices  5.59 us (1%)
    reduce_scatter x1, waiting for transfers between devices, on_device(): lax.psum_scatter(folded_term, 'pa', scatter_dimension=2, tiled=True)  92 us
    reduce_scatter x1, waiting for transfers between devices, on_device(): lax.psum_scatter(second_term, 'pa', scatter_dimension=2, tiled=True)  90.1 us
    all_gather x1, waiting for transfers between devices, on_device(): whole_current = lax.all_gather(current, 'pa', axis=2, tiled=True)  81.5 us
    all_to_all x1, blocking collectives, balance_hubs(): lax.all_to_all(jnp.stack(history, 0), axis_name, 0, 0)  51.1 us
    all_to_all x2, blocking collectives, kernel_product(): lax.all_to_all(screened, 'ka', split_axis=0, concat_axis=1, tiled=True)  30.6 us
    all_to_all x1, blocking collectives, kernel_product(): lax.all_to_all(pair_blocks, 'ka', split_axis=1, concat_axis=0, tiled=True)  18.5 us
    unnamed x30, local copies, waits for them, and re-layouts  9.31 us
  transfers between devices with their start and end apart: 4, of which 4 were waited for; matrix products, arithmetic and copies ran while one was open for 0% of the time, Pallas kernels for 0%

profile of v1, /device:TPU:8, one launch (start us, length us, event | category | flops | bytes accessed | tf_op | source)
XLA Modules:
  0.0 455.5 jit_solution(15434855989084327053)
XLA Ops:
  7.2 0.0 copy-start
  7.2 0.0 all-gather.2.cloned.1.call-start
  7.2 0.7 all-gather.2.cloned.1.call-update
  7.9 81.5 %all-gather.2.cloned.1.call-done = f32[8,256,256]{1,2,0:T(8,128)} async-done(((f32[8,256,32]{1,2,0:T(8,128)}), f32[8,256,256]{1,2,0:T(8,128)}) %all-gather.2.cloned.1.call-update) | async-done | bytes 2097168 | tf_op jit(solution)/shard_map/all_gather | solution.py:55
  89.4 3.0 fusion.60
  92.4 1.3 convolution_bitcast_fusion.3
  93.7 0.4 copy.34
  94.1 1.2 reshape.81
  95.2 5.2 %all-to-all-start = ((f32[32,1,2048]{2,1,0:T(1,128)}), f32[32,1,2048]{2,1,0:T(1,128)S(1)}, u32[]{:S(2)}, u32[]{:S(2)}) async-start(f32[32,1,2048]{2,1,0:T(1,128)} %reshape.81), calls=%async_computation | async-start | bytes 524288 | tf_op jit(solution)/shard_map/all_to_all | solution.py:45
  100.4 0.3 reduce-scatter.3.cloned.1.call-start
  100.8 1.8 copy.37
  102.6 7.3 %all-to-all-done = f32[32,1,2048]{2,1,0:T(1,128)S(1)} async-done(((f32[32,1,2048]{2,1,0:T(1,128)}), f32[32,1,2048]{2,1,0:T(1,128)S(1)}, u32[]{:S(2)}, u32[]{:S(2)}) %all-to-all-start) | async-done | bytes 262176 | tf_op jit(solution)/shard_map/all_to_all | solution.py:45
  109.8 0.6 broadcast.136
  110.4 1.2 reduce
  111.6 0.3 reshape.82
  112.0 0.0 copy-start.9
  112.0 1.2 copy.36
  113.2 1.5 reshape.75
  114.7 1.6 convolution_multiply_fusion.2
  116.3 1.6 convolution_multiply_fusion.3
  117.8 1.7 fusion.19
  119.5 1.7 fusion.1
  121.2 0.4 copy.39
  121.7 0.0 copy-start.1
  121.7 1.2 reshape.83
  122.8 15.4 %all_to_all.71 = f32[32,1,2048]{2,1,0:T(1,128)S(1)} all-to-all(f32[32,1,2048]{2,1,0:T(1,128)} %reshape.83), channel_id=1, replica_groups=mesh['ka'=32,'pa'=8] {'ka'}, dimensions={0} | all-to-all | bytes 524288 | tf_op jit(solution)/shard_map/all_to_all | solution.py:48
  138.3 2.0 reduce.1
  140.2 1.3 reshape.84
  141.5 1.9 fusion.4
  143.4 3.5 convolution_bitcast_fusion.1
  146.9 0.0 reduce-scatter.3.cloned.1.call-update
  146.9 0.0 reduce-scatter.5.cloned.1.call-start
  146.9 92.0 %reduce-scatter.3.cloned.1.call-done = f32[8,256,32]{1,2,0:T(8,128)} async-done(((f32[8,256,256]{1,2,0:T(8,128)}), f32[8,256,32]{1,2,0:T(8,128)}) %reduce-scatter.3.cloned.1.call-update) | async-done | bytes 262160 | tf_op jit(solution)/shard_map/reduce_scatter | solution.py:59
  239.0 1.0 multiply_subtract_fusion.1
  240.0 0.0 copy-start.2
  240.0 0.2 stack.2
  240.3 0.4 copy-done.2
  240.7 51.1 %all_to_all.72 = f32[8,8,256,32]{2,3,1,0:T(8,128)S(1)} all-to-all(f32[8,8,256,32]{2,3,1,0:T(8,128)S(1)} %stack.2), channel_id=1, replica_groups=mesh['ka'=32,'pa'=8] {'pa'}, dimensions={0} | all-to-all | bytes 4194304 | tf_op jit(solution)/shard_map/all_to_all | solution.py:14
  291.8 0.2 copy.43
  292.0 1.4 fusion.61
  293.4 2.0 convolution_bitcast_fusion.2
  295.4 1.4 copy.45
  296.8 1.2 reshape.85
  297.9 18.5 %all_to_all.73 = f32[32,1,2048]{2,1,0:T(1,128)S(1)} all-to-all(f32[32,1,2048]{2,1,0:T(1,128)} %reshape.85), channel_id=1, replica_groups=mesh['ka'=32,'pa'=8] {'ka'}, dimensions={0} | all-to-all | bytes 524288 | tf_op jit(solution)/shard_map/all_to_all | solution.py:45
  316.4 2.0 reduce.2
  318.4 1.3 reshape.86
  319.7 1.2 copy.47
  320.9 1.6 reshape.79
  322.4 2.5 convolution_multiply_fusion
  325.0 0.0 copy-done.10
  325.0 1.6 convolution_multiply_fusion.1
  326.6 1.7 fusion.16
  328.2 2.4 fusion
  330.6 1.4 copy.50
  332.0 1.2 reshape.87
  333.2 15.1 %all_to_all.74 = f32[32,1,2048]{2,1,0:T(1,128)S(1)} all-to-all(f32[32,1,2048]{2,1,0:T(1,128)} %reshape.87), channel_id=1, replica_groups=mesh['ka'=32,'pa'=8] {'ka'}, dimensions={0} | all-to-all | bytes 524288 | tf_op jit(solution)/shard_map/all_to_all | solution.py:48
  348.3 2.0 reduce.3
  350.3 1.3 reshape.88
  351.6 1.9 fusion.2
  353.4 3.5 convolution_bitcast_fusion
  356.9 0.0 reduce-scatter.5.cloned.1.call-update
  356.9 90.1 %reduce-scatter.5.cloned.1.call-done = f32[8,256,32]{1,2,0:T(8,128)} async-done(((f32[8,256,256]{1,2,0:T(8,128)}), f32[8,256,32]{1,2,0:T(8,128)}) %reduce-scatter.5.cloned.1.call-update) | async-done | bytes 262160 | tf_op jit(solution)/shard_map/reduce_scatter | solution.py:63
  447.0 0.0 copy-done.3
  447.0 1.7 multiply_subtract_fusion
  (16 shorter events, 0.0 us)
Async XLA Ops:
  7.2 85.2 %copy-start = (f32[8,256,256]{2,1,0:T(8,128)S(1)}, f32[8,256,256]{2,1,0:T(8,128)}, u32[]{:S(2)}) copy-start(f32[8,256,256]{2,1,0:T(8,128)} %param.9) | copy-start | bytes 6291460
  7.2 82.2 %all-gather.2.cloned.1.call-start = ((), (), s32[]{:S(2)}) async-start(), calls=%async_computation.7 | async-start | bytes 2359296 | tf_op jit(solution)/shard_map/all_gather | solution.py:55
  95.2 14.6 %all-to-all-start = ((f32[32,1,2048]{2,1,0:T(1,128)}), f32[32,1,2048]{2,1,0:T(1,128)S(1)}, u32[]{:S(2)}, u32[]{:S(2)}) async-start(f32[32,1,2048]{2,1,0:T(1,128)} %reshape.81), calls=%async_computation | async-start | bytes 524288 | tf_op jit(solution)/shard_map/all_to_all | solution.py:45
  100.4 138.5 %reduce-scatter.3.cloned.1.call-start = ((), (), s32[]{:S(2)}) async-start(), calls=%async_computation.8 | async-start | bytes 2359296 | tf_op jit(solution)/shard_map/reduce_scatter | solution.py:59
  112.0 2.7 copy-start.9
  121.7 19.9 %copy-start.1 = (f32[8,256,32]{1,2,0:T(8,128)S(1)}, f32[8,256,32]{1,2,0:T(8,128)}, u32[]{:S(2)}) copy-start(f32[8,256,32]{1,2,0:T(8,128)} %param.10) | copy-start | bytes 786436
  146.8 92.1 %copy-start.4 = (f32[8,256,32]{1,2,0:T(8,128)S(1)}, f32[8,256,32]{1,2,0:T(8,128)}, u32[]{:S(2)}) copy-start(f32[8,256,32]{1,2,0:T(8,128)} %param.7) | copy-start | bytes 786436
  146.8 92.1 %copy-start.6 = (f32[8,256,32]{1,2,0:T(8,128)S(1)}, f32[8,256,32]{1,2,0:T(8,128)}, u32[]{:S(2)}) copy-start(f32[8,256,32]{1,2,0:T(8,128)} %param.8) | copy-start | bytes 786436
  146.9 92.1 %copy-start.8 = (f32[8,256,32]{1,2,0:T(8,128)S(1)}, f32[8,256,32]{1,2,0:T(8,128)}, u32[]{:S(2)}) copy-start(f32[8,256,32]{1,2,0:T(8,128)} %param.6) | copy-start | bytes 786436
  146.9 300.1 %reduce-scatter.5.cloned.1.call-start = ((), (), s32[]{:S(2)}) async-start(), calls=%async_computation.9 | async-start | bytes 2359296 | tf_op jit(solution)/shard_map/reduce_scatter | solution.py:63
  240.0 0.7 copy-start.2
  320.9 4.1 copy-start.10
  356.9 90.1 %copy-start.3 = (f32[8,256,32]{1,2,0:T(8,128)S(1)}, f32[8,256,32]{1,2,0:T(8,128)}, u32[]{:S(2)}) copy-start(f32[8,256,32]{1,2,0:T(8,128)} %copy-done.2) | copy-start | bytes 786436
  356.9 90.1 %copy-start.5 = (f32[8,256,32]{1,2,0:T(8,128)S(1)}, f32[8,256,32]{1,2,0:T(8,128)}, u32[]{:S(2)}) copy-start(f32[8,256,32]{1,2,0:T(8,128)} %param.7) | copy-start | bytes 786436
  356.9 90.1 %copy-start.7 = (f32[8,256,32]{1,2,0:T(8,128)S(1)}, f32[8,256,32]{1,2,0:T(8,128)}, u32[]{:S(2)}) copy-start(f32[8,256,32]{1,2,0:T(8,128)} %param.8) | copy-start | bytes 786436
Sparse Core Ops, SparseCore 0:
  10.6 78.7 all-gather.1
  147.0 91.9 reduce-scatter.2
  357.0 89.9 reduce-scatter.4
